TPU v7x, 32 devices: a whole 2x2x4 slice. The times are simulated.
32 devices in a mesh: groups: 2 (over x), dp: 8 (over z, y), tensor: 2 (over core).
Axes of the slice: x: 2, y: 2, z: 4, core: 2. Of those that a mesh axis runs over, the one named last changes fastest.
Arguments:
- x_in: bfloat16 [1536, 8192], P(('groups', 'dp'), 'tensor'), parts along dimension 0, may hold values from -6 to 6
- gate_pre: bfloat16 [1536, 28672], P(('groups', 'dp'), 'tensor'), parts along dimension 0, may hold values from -6 to 6
- up_pre: bfloat16 [1536, 28672], P(('groups', 'dp'), 'tensor'), parts along dimension 0, may hold values from -6 to 6
- grad_hidden: bfloat16 [1536, 28672], P(('groups', 'dp'), 'tensor'), parts along dimension 0, may hold values from -6 to 6
- grad_out: bfloat16 [1536, 8192], P(('groups', 'dp'), 'tensor'), parts along dimension 0, may hold values from -6 to 6
- proj_model: bfloat16 [64, 8192], P('dp', 'tensor'), may hold values from -0.0625 to 0.0625
- proj_hidden: bfloat16 [64, 28672], P('dp', 'tensor'), may hold values from -0.03125 to 0.03125
- lengths: int32 [8], P('groups'), parts along dimension 0, may hold values from 1 to 384, 768 in all
- queries: bfloat16 [512, 12288], P(('groups', 'dp'), 'tensor'), parts along dimension 0, may hold values from -0.0546875 to 0.0546875
- cand: int32 [8, 8], P('groups'), parts along dimension 0, may hold values from 0 to 7
- cand_count: int32 [8], P('groups'), parts along dimension 0, may hold values from 1 to 8
Outputs:
- scores: float32 [8, 8, 32], P('groups'), parts along dimension 0
There are 2 independent parts, one for each index of `groups`. A program takes and returns all parts, laid end to end along the dimension named above; an argument that names none is the same for every part. Nothing has to cross between parts.
Inputs may be any that keep to these rules, and one draw needn't show every extreme that they name: The lengths sum to 768; sequence s occupies the tokens that follow those of sequences 0 to s - 1.
All inputs are finite; a program needn't handle non-finite values.
Results may differ from a plain program's by a relative error of at most 0.0042.
Values may be sent and summed in bfloat16 or wider, within the bound.
No kernel may reach another device: no remote copies, remote signals or barrier semaphores. Data moves between devices by JAX's collectives and lax.ppermute only.
A program may use at most 64 MiB of HBM per device.

v0:
```python
import jax
import jax.numpy as jnp
from jax import lax
from jax.sharding import PartitionSpec as P

QBS = 32
CAND = 8


def contract_rows(left, right):
    return lax.dot_general(
        left, right, (((1,), (1,)), ((), ())), preferred_element_type=jnp.float32
    )


def local(
    x_in,
    gate_pre,
    up_pre,
    grad_hidden,
    grad_out,
    proj_model,
    proj_hidden,
    lengths,
    queries,
    cand,
    cand_count,
):
    model_rows, hidden_rows = (
        lax.all_gather(proj_model, "dp", axis=0, tiled=True),
        lax.all_gather(proj_hidden, "dp", axis=0, tiled=True),
    )
    gate_f = gate_pre.astype(jnp.float32)
    up_f = up_pre.astype(jnp.float32)
    grad_f = grad_hidden.astype(jnp.float32)
    sig_gate = jax.nn.sigmoid(gate_f)
    hidden_act = (gate_f * sig_gate * up_f).astype(jnp.bfloat16)
    grad_gate = (grad_f * up_f * sig_gate * (1.0 + gate_f * (1.0 - sig_gate))).astype(jnp.bfloat16)
    grad_up = (grad_f * gate_f * sig_gate).astype(jnp.bfloat16)
    partial_proj = jnp.concatenate(
        [
            contract_rows(x_in, model_rows),
            contract_rows(hidden_act, hidden_rows),
            contract_rows(grad_gate, hidden_rows),
            contract_rows(grad_up, hidden_rows),
            contract_rows(grad_out, model_rows),
        ],
        axis=1,
    )
    summed = lax.psum(partial_proj, "tensor")
    rank_size = model_rows.shape[0]
    half_rank = rank_size // lax.axis_size("tensor")
    core_index = lax.axis_index("tensor")
    model_proj = summed[:, 0:rank_size]
    hidden_proj = summed[:, rank_size : 2 * rank_size]
    gate_proj = summed[:, 2 * rank_size : 3 * rank_size]
    up_proj = summed[:, 3 * rank_size : 4 * rank_size]
    out_proj = summed[:, 4 * rank_size : 5 * rank_size]
    seq_count = lengths.shape[0]
    tok_count = x_in.shape[0]
    position = lax.axis_index("dp") * tok_count + jnp.arange(tok_count, dtype=jnp.int32)
    seq_ends = jnp.cumsum(lengths)
    seq_of = jnp.sum((seq_ends[None, :] <= position[:, None]).astype(jnp.int32), axis=1)
    onehot = (seq_of[:, None] == jnp.arange(seq_count, dtype=jnp.int32)[None, :]).astype(
        jnp.float32
    )

    def gram_sum(out_vecs, in_vecs):
        own_rows = lax.dynamic_slice_in_dim(out_vecs, core_index * half_rank, half_rank, 1)
        left = (onehot[:, :, None] * own_rows[:, None, :]).reshape(tok_count, seq_count * half_rank)
        return jnp.dot(left.T, in_vecs, precision=lax.Precision.HIGHEST).reshape(
            seq_count, half_rank, rank_size
        )

    partial_grads = jnp.stack(
        [
            gram_sum(gate_proj, model_proj),
            gram_sum(up_proj, model_proj),
            gram_sum(out_proj, hidden_proj),
        ],
        axis=2,
    )
    partial_grads = partial_grads.reshape(seq_count, half_rank * 3 * rank_size)
    slice_sums = lax.psum_scatter(partial_grads, "dp", scatter_dimension=1, tiled=True)
    slice_grads = slice_sums.astype(jnp.bfloat16)
    scale_rows = 1.0 / jnp.sqrt(lengths.astype(jnp.float32))[:, None]
    query_slice = lax.all_to_all(queries, "dp", split_axis=1, concat_axis=0, tiled=True)
    score_part = contract_rows(slice_grads, query_slice)
    full = lax.psum(score_part, ("dp", "tensor")) * scale_rows
    blocks = full.reshape(seq_count, -1, QBS)
    block_number = blocks.shape[1]
    picker = (cand[:, :, None] == jnp.arange(block_number, dtype=jnp.int32)[None, None, :]).astype(
        jnp.float32
    )
    chosen = jnp.einsum("scb,sbk->sck", picker, blocks, precision=lax.Precision.HIGHEST)
    in_use = jnp.arange(CAND, dtype=jnp.int32)[None, :] < cand_count[:, None]
    return jnp.where(in_use[:, :, None], chosen, jnp.float32(0.0))


def solution(mesh):
    placed = (
        P(("groups", "dp"), "tensor"),
        P(("groups", "dp"), "tensor"),
        P(("groups", "dp"), "tensor"),
        P(("groups", "dp"), "tensor"),
        P(("groups", "dp"), "tensor"),
        P("dp", "tensor"),
        P("dp", "tensor"),
        P("groups"),
        P(("groups", "dp"), "tensor"),
        P("groups", None),
        P("groups"),
    )
    return jax.shard_map(
        local, mesh=mesh, in_specs=placed, out_specs=P("groups", None, None), check_vma=False
    )
```

profile of v0, /device:TPU:0, one launch (start us, length us, event | category | flops | bytes accessed | tf_op | source)
XLA Modules:
  0.0 216.5 jit_solution(13726743882510743481)
XLA Ops:
  6.5 0.7 all-gather.2.cloned.1.call-update
  7.3 1.8 copy.25
  9.0 7.3 %all-to-all-start = ((bf16[32,8,768]{2,0,1:T(8,128)(2,1)}), bf16[32,8,768]{2,0,1:T(8,128)(2,1)S(1)}, u32[]{:S(2)}, u32[]{:S(2)}) async-start(bf16[32,8,768]{2,0,1:T(8,128)(2,1)} %bitcast.56), calls=%async_computation | async-start | bytes 786432 | tf_op jit(solution)/shard_map/all_to_all | solution.py:87
  16.3 0.0 all-reduce.2.cloned.1.call-start
  16.4 0.8 reduce-window.8
  17.2 0.1 convert_reduce_fusion
  17.3 40.1 %all_gather.6 = bf16[64,4096]{1,0:T(8,128)(2,1)S(1)} all-gather(bf16[8,4096]{1,0:T(8,128)(2,1)} %param.16), channel_id=1, replica_groups=mesh['groups'=2,'dp'=8,'tensor'=2] {'dp'}, dimensions={0}, use_global_device_ids=true | all-gather | bytes 589824 | tf_op jit(solution)/shard_map/all_gather | solution.py:30
  57.4 0.4 convolution_dynamic-update-slice_fusion.1
  57.8 8.1 %all-gather.2.cloned.1.call-done = bf16[64,14336]{1,0:T(8,128)(2,1)} async-done(((bf16[8,14336]{1,0:T(8,128)(2,1)}), bf16[64,14336]{1,0:T(8,128)(2,1)}) %all-gather.2.cloned.1.call-update) | async-done | bytes 1835024 | tf_op jit(solution)/shard_map/all_gather | solution.py:31
  65.9 5.0 %fusion.19 = f32[96,320]{0,1:T(8,128)S(1)} fusion(f32[96,320]{0,1:T(8,128)S(1)} %convolution_dynamic-update-slice_fusion.1, bf16[64,14336]{1,0:T(8,128)(2,1)} %all-gather.2.cloned.1.call-done, bf16[96,14336]{1,0:T(8,128)(2,1)} %param.13, bf16[96,14336]{1,0:T(8,128)(2,1)} %param.12), kind=kOutput, calls=%fused_computation.25 | convolution fusion | flops 187170816 | bytes 7372800 | tf_op jit(solution)/shard_map/dot_general | solution.py:11
  70.9 0.5 copy-done.5
  71.5 0.5 copy-done.6
  72.0 2.6 %fusion.16 = f32[96,320]{0,1:T(8,128)S(1)} fusion(f32[96,320]{0,1:T(8,128)S(1)} %fusion.19, bf16[64,14336]{1,0:T(8,128)(2,1)S(1)} %copy-done.6, bf16[96,14336]{1,0:T(8,128)(2,1)S(1)} %copy-done.3, bf16[96,14336]{1,0:T(8,128)(2,1)S(1)} %copy-done.5, bf16[96,14336]{1,0:T(8,128)(2,1)S(1)} %copy-done.4), kind=kOutput, calls=%fused_computation.24 | convolution fusion | flops 194052096 | bytes 10125312 | tf_op jit(solution)/shard_map/dot_general | solution.py:11
  74.6 1.8 fusion.22
  76.4 0.4 convolution_dynamic-update-slice_fusion
  76.8 0.7 copy-done.2
  77.5 0.0 all-reduce.2.cloned.1.call-update
  77.5 0.0 reduce-scatter.4.cloned.1.call-start
  77.5 17.6 %all-reduce.2.cloned.1.call-done = f32[96,320]{0,1:T(8,128)} async-done(((f32[96,320]{0,1:T(8,128)}), f32[96,320]{0,1:T(8,128)}) %all-reduce.2.cloned.1.call-update) | async-done | bytes 122896 | tf_op jit(solution)/shard_map/psum | solution.py:50
  95.1 0.8 fusion.44
  96.0 1.0 convolution_bitcast_fusion.1
  96.9 1.0 convolution_bitcast_fusion
  97.9 1.0 convolution_bitcast_fusion.2
  98.9 2.3 %copy.21 = f32[4,32,3,64]{0,3,2,1:T(8,128)} copy(f32[4,32,3,64]{3,1,0,2:T(8,128)S(1)} %pad_maximum_fusion) | data formatting | bytes 196608
  101.2 0.1 iota_compare_fusion.3
  101.3 75.5 %reduce-scatter.4.cloned.1.call-done = f32[768,4]{1,0:T(8,128)} async-done(((f32[6144,4]{1,0:T(8,128)}), f32[768,4]{1,0:T(8,128)}) %reduce-scatter.4.cloned.1.call-update) | async-done | bytes 12304
  176.8 1.1 copy.20
  178.0 0.2 fusion.45
  178.1 30.8 %psum.15 = f32[4,256]{1,0:T(4,128)S(1)} all-reduce(f32[4,256]{1,0:T(4,128)S(1)} %fusion.45), channel_id=1, replica_groups=mesh['groups'=2,'dp'=8,'tensor'=2] {'dp','tensor'}, use_global_device_ids=true, to_apply=%region_4.5 | all-reduce | flops 1024 | bytes 8192 | tf_op jit(solution)/shard_map/psum | solution.py:89
  209.0 0.1 broadcast_multiply_fusion
  209.0 0.1 reshape.116
  209.1 0.8 convolution_select_fusion
  (26 shorter events, 0.1 us)
Async XLA Ops:
  6.5 50.8 %copy-start = (bf16[96,4096]{1,0:T(8,128)(2,1)S(1)}, bf16[96,4096]{1,0:T(8,128)(2,1)}, u32[]{:S(2)}) copy-start(bf16[96,4096]{1,0:T(8,128)(2,1)} %param.11) | copy-start | bytes 2359300
  6.5 59.4 %all-gather.2.cloned.1.call-start = ((), (), s32[]{:S(2)}) async-start(), calls=%async_computation.2 | async-start | bytes 2064384 | tf_op jit(solution)/shard_map/all_gather | solution.py:31
  9.0 168.9 %all-to-all-start = ((bf16[32,8,768]{2,0,1:T(8,128)(2,1)}), bf16[32,8,768]{2,0,1:T(8,128)(2,1)S(1)}, u32[]{:S(2)}, u32[]{:S(2)}) async-start(bf16[32,8,768]{2,0,1:T(8,128)(2,1)} %bitcast.56), calls=%async_computation | async-start | bytes 786432 | tf_op jit(solution)/shard_map/all_to_all | solution.py:87
  16.3 78.8 %all-reduce.2.cloned.1.call-start = ((), (), s32[]{:S(2)}) async-start(), calls=%async_computation.3 | async-start | bytes 327680 | tf_op jit(solution)/shard_map/psum | solution.py:50
  65.9 5.0 %copy-start.3 = (bf16[96,14336]{1,0:T(8,128)(2,1)S(1)}, bf16[96,14336]{1,0:T(8,128)(2,1)}, u32[]{:S(2)}) copy-start(bf16[96,14336]{1,0:T(8,128)(2,1)} %param.13) | copy-start | bytes 8257540
  65.9 5.0 %copy-start.4 = (bf16[96,14336]{1,0:T(8,128)(2,1)S(1)}, bf16[96,14336]{1,0:T(8,128)(2,1)}, u32[]{:S(2)}) copy-start(bf16[96,14336]{1,0:T(8,128)(2,1)} %param.12) | copy-start | bytes 8257540
  65.9 5.6 %copy-start.5 = (bf16[96,14336]{1,0:T(8,128)(2,1)S(1)}, bf16[96,14336]{1,0:T(8,128)(2,1)}, u32[]{:S(2)}) copy-start(bf16[96,14336]{1,0:T(8,128)(2,1)} %param.14) | copy-start | bytes 8257540
  65.9 6.1 %copy-start.6 = (bf16[64,14336]{1,0:T(8,128)(2,1)S(1)}, bf16[64,14336]{1,0:T(8,128)(2,1)}, u32[]{:S(2)}) copy-start(bf16[64,14336]{1,0:T(8,128)(2,1)} %all-gather.2.cloned.1.call-done) | copy-start | bytes 5505028
  74.6 1.8 copy-start.1
  74.6 2.9 %copy-start.8 = (s32[4]{0:T(128)S(1)}, s32[4]{0:T(128)}, u32[]{:S(2)}) copy-start(s32[4]{0:T(128)} %param.18) | copy-start | bytes 52
  76.8 0.7 copy-start.2
  77.5 99.3 %reduce-scatter.4.cloned.1.call-start = ((), (), s32[]{:S(2)}) async-start(), calls=%async_computation.4 | async-start | bytes 3538944
  98.9 2.3 %copy-start.9 = (s32[4]{0:T(128)S(1)}, s32[4]{0:T(128)}, u32[]{:S(2)}) copy-start(s32[4]{0:T(128)} %param.21) | copy-start | bytes 52
  98.9 110.2 %copy-start.7 = (s32[4,8]{1,0:T(4,128)S(1)}, s32[4,8]{1,0:T(4,128)}, u32[]{:S(2)}) copy-start(s32[4,8]{1,0:T(4,128)} %param.20) | copy-start | bytes 388
Sparse Core Ops, SparseCore 0:
  9.5 56.3 all-gather.1
  77.6 17.4 all-reduce.1
  101.4 75.4 reduce-scatter.3
where the time goes:
time: 217 us; the launch traced here: 216 us
  waiting for transfers between devices  102 us (47%)
  blocking collectives  70.9 us (33%)
  matrix products  14 us (6%)
  between operations  13.3 us (6%)
  local copies, waits for them, and re-layouts  7.85 us (4%)
  starting transfers between devices  7.39 us (3%)
    unnamed x4, waiting for transfers between devices  76.2 us
    all_gather x1, blocking collectives, local(): lax.all_gather(proj_model, 'dp', axis=0, tiled=True)  40.1 us
    psum x1, blocking collectives, local(): full = lax.psum(score_part, ('dp', 'tensor')) * scale_rows  30.8 us
    psum x1, waiting for transfers between devices, local(): summed = lax.psum(partial_proj, 'tensor')  17.6 us
    dot_general x6, matrix products, contract_rows(): lax.dot_general(left, right, (((1,), (1,)), ((), ())), preferred_element_...  10.3 us
    all_gather x1, waiting for transfers between devices, local(): lax.all_gather(proj_hidden, 'dp', axis=0, tiled=True)  8.12 us
    all_to_all x1, starting transfers between devices, local(): lax.all_to_all(queries, 'dp', split_axis=1, concat_axis=0, tiled=True)  7.31 us
    unnamed x22, local copies, waits for them, and re-layouts  5.18 us
  transfers between devices with their start and end apart: 4, of which 3 were waited for; matrix products, arithmetic and copies ran while one was open for 9% of the time, Pallas kernels for 0%

commit v1 on v0

--- a/solution.py
+++ b/solution.py
@@ -47,7 +47,7 @@
         ],
         axis=1,
     )
-    summed = lax.psum(partial_proj, "tensor")
+    summed = jnp.sum(lax.all_gather(partial_proj, "tensor"), axis=0)
     rank_size = model_rows.shape[0]
     half_rank = rank_size // lax.axis_size("tensor")
     core_index = lax.axis_index("tensor")

time: 217 us -> 196 us (0.903)
  waiting for transfers between devices: 102 us -> 82.5 us
  matrix products: 14 us -> 11.8 us
    psum x1 -> x0, waiting for transfers between devices: 17.6 us -> none  [local(): summed = lax.psum(partial_proj, 'tensor')]
    dot_general x3, matrix products: 2.89 us -> 0.69 us  [gram_sum(): jnp.dot(left.T, in_vecs, precision=lax.Precision.HIGHEST)]
    unnamed x4 -> x3, waiting for transfers between devices: 76.2 us -> 74.3 us
    unnamed x22 -> x18, local copies, waits for them, and re-layouts: 5.18 us -> 4.52 us
  transfers between devices with their start and end apart: 4 -> 3, of which waited for: 3 -> 2; matrix products, arithmetic and copies ran while one was open for 9% -> 9% of each run, Pallas kernels for 0% -> 0%
where the time goes in v1:
time: 196 us
  waiting for transfers between devices  82.5 us (42%)
  blocking collectives  72.2 us (37%)
  between operations  13.5 us (7%)
  matrix products  11.8 us (6%)
  starting transfers between devices  7.35 us (4%)
  local copies, waits for them, and re-layouts  6.96 us (4%)
    unnamed x3, waiting for transfers between devices  74.3 us
    all_gather x1, blocking collectives, local(): lax.all_gather(proj_model, 'dp', axis=0, tiled=True)  39.4 us
    psum x1, blocking collectives, local(): full = lax.psum(score_part, ('dp', 'tensor')) * scale_rows  30.8 us
    dot_general x6, matrix products, contract_rows(): lax.dot_general(left, right, (((1,), (1,)), ((), ())), preferred_element_...  10.3 us
    all_gather x1, waiting for transfers between devices, local(): lax.all_gather(proj_hidden, 'dp', axis=0, tiled=True)  8.13 us
    all_to_all x1, starting transfers between devices, local(): lax.all_to_all(queries, 'dp', split_axis=1, concat_axis=0, tiled=True)  7.31 us
    unnamed x18, local copies, waits for them, and re-layouts  4.52 us
  transfers between devices with their start and end apart: 3, of which 2 were waited for; matrix products, arithmetic and copies ran while one was open for 9% of the time, Pallas kernels for 0%

profile of v1, /device:TPU:0, one launch (start us, length us, event | category | flops | bytes accessed | tf_op | source)
XLA Modules:
  0.0 196.1 jit_solution(11970745151753633473)
XLA Ops:
  6.5 0.7 all-gather.3.cloned.1.call-update
  7.3 1.8 copy.41
  9.0 7.3 %all-to-all-start = ((bf16[32,8,768]{2,0,1:T(8,128)(2,1)}), bf16[32,8,768]{2,0,1:T(8,128)(2,1)S(1)}, u32[]{:S(2)}, u32[]{:S(2)}) async-start(bf16[32,8,768]{2,0,1:T(8,128)(2,1)} %bitcast.60), calls=%async_computation | async-start | bytes 786432 | tf_op jit(solution)/shard_map/all_to_all | solution.py:87
  16.4 0.8 reduce-window.8
  17.2 0.1 convert_reduce_fusion
  17.3 0.7 convert_rsqrt_fusion
  18.0 39.4 %all_gather.12 = bf16[64,4096]{1,0:T(8,128)(2,1)S(1)} all-gather(bf16[8,4096]{1,0:T(8,128)(2,1)} %param.16), channel_id=1, replica_groups=mesh['groups'=2,'dp'=8,'tensor'=2] {'dp'}, dimensions={0}, use_global_device_ids=true | all-gather | bytes 589824 | tf_op jit(solution)/shard_map/all_gather | solution.py:30
  57.4 0.4 convolution_dynamic-update-slice_fusion.1
  57.8 8.1 %all-gather.3.cloned.1.call-done = bf16[64,14336]{1,0:T(8,128)(2,1)} async-done(((bf16[8,14336]{1,0:T(8,128)(2,1)}), bf16[64,14336]{1,0:T(8,128)(2,1)}) %all-gather.3.cloned.1.call-update) | async-done | bytes 1835024 | tf_op jit(solution)/shard_map/all_gather | solution.py:31
  65.9 5.0 %fusion.19 = f32[96,320]{0,1:T(8,128)S(1)} fusion(f32[96,320]{0,1:T(8,128)S(1)} %convolution_dynamic-update-slice_fusion.1, bf16[64,14336]{1,0:T(8,128)(2,1)} %all-gather.3.cloned.1.call-done, bf16[96,14336]{1,0:T(8,128)(2,1)} %param.13, bf16[96,14336]{1,0:T(8,128)(2,1)} %param.12), kind=kOutput, calls=%fused_computation.25 | convolution fusion | flops 187170816 | bytes 7372800 | tf_op jit(solution)/shard_map/dot_general | solution.py:11
  70.9 0.6 copy-done.4
  71.5 0.5 copy-done.5
  72.0 2.6 %fusion.16 = f32[96,320]{0,1:T(8,128)S(1)} fusion(f32[96,320]{0,1:T(8,128)S(1)} %fusion.19, bf16[64,14336]{1,0:T(8,128)(2,1)S(1)} %copy-done.5, bf16[96,14336]{1,0:T(8,128)(2,1)S(1)} %copy-done.2, bf16[96,14336]{1,0:T(8,128)(2,1)S(1)} %copy-done.4, bf16[96,14336]{1,0:T(8,128)(2,1)S(1)} %copy-done.3), kind=kOutput, calls=%fused_computation.24 | convolution fusion | flops 194052096 | bytes 10125312 | tf_op jit(solution)/shard_map/dot_general | solution.py:11
  74.6 1.8 fusion.22
  76.4 0.4 convolution_dynamic-update-slice_fusion
  76.8 0.1 copy.25
  76.9 2.0 %all-gather = f32[192,320]{1,0:T(8,128)S(1)} all-gather(f32[96,320]{1,0:T(8,128)S(1)} %copy.25), channel_id=2, replica_groups=mesh['groups'=2,'dp'=8,'tensor'=2] {'tensor'}, dimensions={0}, use_global_device_ids=true | all-gather | bytes 368640 | tf_op jit(solution)/shard_map/all_gather | solution.py:50
  78.9 0.1 fusion.44
  79.0 0.1 constant_dynamic-slice_fusion
  79.1 0.1 constant_dynamic-slice_fusion.2
  79.3 0.1 copy.29
  79.3 0.1 copy.26
  79.4 0.2 convolution_bitcast_fusion.1
  79.6 0.3 convolution_bitcast_fusion
  79.9 0.2 convolution_bitcast_fusion.2
  80.2 2.3 %copy.35 = f32[4,32,3,64]{0,3,2,1:T(8,128)} copy(f32[4,32,3,64]{3,1,0,2:T(8,128)S(1)} %pad_maximum_fusion) | data formatting | bytes 196608
  82.6 73.6 %reduce-scatter.4.cloned.1.call-done = f32[768,4]{1,0:T(8,128)} async-done(((f32[6144,4]{1,0:T(8,128)}), f32[768,4]{1,0:T(8,128)}) %reduce-scatter.4.cloned.1.call-update) | async-done | bytes 12304
  156.2 1.1 copy.34
  157.3 0.2 fusion.45
  157.5 30.8 %psum.7 = f32[4,256]{1,0:T(4,128)S(1)} all-reduce(f32[4,256]{1,0:T(4,128)S(1)} %fusion.45), channel_id=1, replica_groups=mesh['groups'=2,'dp'=8,'tensor'=2] {'dp','tensor'}, use_global_device_ids=true, to_apply=%region_4.5 | all-reduce | flops 1024 | bytes 8192 | tf_op jit(solution)/shard_map/psum | solution.py:89
  188.4 0.1 reshape.116
  188.5 0.8 convolution_select_fusion
  (25 shorter events, 0.3 us)
Async XLA Ops:
  6.5 50.8 %copy-start = (bf16[96,4096]{1,0:T(8,128)(2,1)S(1)}, bf16[96,4096]{1,0:T(8,128)(2,1)}, u32[]{:S(2)}) copy-start(bf16[96,4096]{1,0:T(8,128)(2,1)} %param.11) | copy-start | bytes 2359300
  6.5 59.4 %all-gather.3.cloned.1.call-start = ((), (), s32[]{:S(2)}) async-start(), calls=%async_computation.2 | async-start | bytes 2064384 | tf_op jit(solution)/shard_map/all_gather | solution.py:31
  9.0 148.3 %all-to-all-start = ((bf16[32,8,768]{2,0,1:T(8,128)(2,1)}), bf16[32,8,768]{2,0,1:T(8,128)(2,1)S(1)}, u32[]{:S(2)}, u32[]{:S(2)}) async-start(bf16[32,8,768]{2,0,1:T(8,128)(2,1)} %bitcast.60), calls=%async_computation | async-start | bytes 786432 | tf_op jit(solution)/shard_map/all_to_all | solution.py:87
  16.3 139.8 %reduce-scatter.4.cloned.1.call-start = ((), (), s32[]{:S(2)}) async-start(), calls=%async_computation.3 | async-start | bytes 3538944
  65.9 5.0 %copy-start.2 = (bf16[96,14336]{1,0:T(8,128)(2,1)S(1)}, bf16[96,14336]{1,0:T(8,128)(2,1)}, u32[]{:S(2)}) copy-start(bf16[96,14336]{1,0:T(8,128)(2,1)} %param.13) | copy-start | bytes 8257540
  65.9 5.0 %copy-start.3 = (bf16[96,14336]{1,0:T(8,128)(2,1)S(1)}, bf16[96,14336]{1,0:T(8,128)(2,1)}, u32[]{:S(2)}) copy-start(bf16[96,14336]{1,0:T(8,128)(2,1)} %param.12) | copy-start | bytes 8257540
  65.9 5.6 %copy-start.4 = (bf16[96,14336]{1,0:T(8,128)(2,1)S(1)}, bf16[96,14336]{1,0:T(8,128)(2,1)}, u32[]{:S(2)}) copy-start(bf16[96,14336]{1,0:T(8,128)(2,1)} %param.14) | copy-start | bytes 8257540
  65.9 6.1 %copy-start.5 = (bf16[64,14336]{1,0:T(8,128)(2,1)S(1)}, bf16[64,14336]{1,0:T(8,128)(2,1)}, u32[]{:S(2)}) copy-start(bf16[64,14336]{1,0:T(8,128)(2,1)} %all-gather.3.cloned.1.call-done) | copy-start | bytes 5505028
  74.6 1.8 copy-start.1
  80.2 2.3 %copy-start.7 = (s32[4]{0:T(128)S(1)}, s32[4]{0:T(128)}, u32[]{:S(2)}) copy-start(s32[4]{0:T(128)} %param.21) | copy-start | bytes 52
  80.2 108.3 %copy-start.6 = (s32[4,8]{1,0:T(4,128)S(1)}, s32[4,8]{1,0:T(4,128)}, u32[]{:S(2)}) copy-start(s32[4,8]{1,0:T(4,128)} %param.20) | copy-start | bytes 388
Sparse Core Ops, SparseCore 0:
  9.5 56.3 all-gather.2
  82.6 73.5 reduce-scatter.3
